TPU v7x, 256 devices: a whole 4x4x8 slice. The times are simulated.
256 devices in a mesh: section: 2 (over x_hi), fsdp: 64 (over y, z, x_lo), dp: 2 (over core).
Axes of the slice: x: 4 (x_hi: 2, x_lo: 2; x = x_hi * 2 + x_lo), y: 4, z: 8, core: 2. Of those that a mesh axis runs over, the one named last changes fastest.
Arguments:
- hidden: bfloat16 [4, 512, 8192], P(('section', 'dp'), 'fsdp'), may hold values from -7 to 7
- cotangent: bfloat16 [4, 512, 8192], P(('section', 'dp'), None, 'fsdp'), may hold values from -6 to 6
- seg_ids: int32 [4, 512], P(('section', 'dp')), may hold values from 0 to 8, as said below
- advantage: float32 [4, 8], P(('section', 'dp')), may hold values from -4 to 4
- w_query: bfloat16 [8192, 8192], P('fsdp'), may hold values from -6 to 6
- w_key: bfloat16 [8192, 1024], P('fsdp'), may hold values from -6 to 6
- w_value: bfloat16 [8192, 1024], P('fsdp'), may hold values from -6 to 6
Outputs:
- rollout_query: bfloat16 [8192, 8192], P(None, 'fsdp')
- rollout_key: bfloat16 [8192, 8192], P(None, 'fsdp')
- rollout_value: bfloat16 [8192, 8192], P(None, 'fsdp')
Inputs may be any that keep to these rules, and one draw needn't show every extreme that they name: `seg_ids`: in each block ids never fall; each id below 8 covers 1 to 64 positions, one of them exactly 64, and every id below 8 appears; id 8 marks padding at the block's end.
All inputs are finite; a program needn't handle non-finite values.
Results may differ from a plain program's by a relative error of at most 0.015.
The roundings to bfloat16 on the way count: a program that leaves them out, or rounds other values in their place, can miss the bound.
Values may be sent and summed in bfloat16 or wider, within the bound.
No kernel may reach another device: no remote copies, remote signals or barrier semaphores. Data moves between devices by JAX's collectives and lax.ppermute only.
A program may use at most 64 MiB of HBM per device.

v0:
```python
import jax
import jax.numpy as jnp
from jax import lax
from jax.sharding import Mesh, PartitionSpec as P

D = 8192
HD = 128
RESP = 8
step_rate = 200.0
rope_base = 1000000.0
norm_eps = 1e-06
masked_score = -1e30
YZ = ("y", "zh", "zl")
KH = ("y", "zh")
MEM = ("zl", "core")
X = ("xh", "xl")
FS = ("y", "zh", "zl", "xl")


def rotate(field, cosine_table, sine_table):
    half_width = field.shape[-1] // 2
    lead_half = field[..., :half_width]
    tail_half = field[..., half_width:]
    return jnp.concatenate(
        [
            lead_half * cosine_table - tail_half * sine_table,
            tail_half * cosine_table + lead_half * sine_table,
        ],
        -1,
    )


def angles(seg_row):
    span_count = seg_row.shape[0]
    earlier = jnp.sum((seg_row[None, :] < seg_row[:, None]).astype(jnp.int32), axis=1)
    positions = jnp.arange(span_count, dtype=jnp.int32) - earlier
    frequency = rope_base ** (-jnp.arange(HD // 2, dtype=jnp.float32) * 2.0 / HD)
    phase_grid = positions.astype(jnp.float32)[:, None] * frequency[None, :]
    return (jnp.cos(phase_grid), jnp.sin(phase_grid))


def token_weights(seg_row, advantage_row):
    id_range = jnp.arange(RESP + 1, dtype=jnp.int32)
    onehot = (seg_row[:, None] == id_range[None, :]).astype(jnp.float32)
    counts = jnp.sum(onehot, axis=0)[:RESP]
    per_token = -advantage_row / counts
    return jnp.sum(onehot[:, :RESP] * per_token[None, :], axis=1)


def attend_back(q_rot, k_rot, v_bf, grad_context, allowed):
    score_scale = HD ** (-0.5)
    f32 = jnp.float32
    scores = jnp.einsum("td,ud->tu", q_rot, k_rot, preferred_element_type=f32) * score_scale
    scores = jnp.where(allowed, scores, masked_score)
    row_top = jnp.max(scores, axis=-1, keepdims=True)
    exponent = jnp.exp(scores - row_top)
    attention = exponent / jnp.sum(exponent, axis=-1, keepdims=True)
    attention_bf = attention.astype(jnp.bfloat16)
    grad_prob = jnp.einsum("td,ud->tu", grad_context, v_bf, preferred_element_type=f32)
    inner_sum = jnp.sum(attention * grad_prob, axis=-1, keepdims=True)
    dscore = (attention * (grad_prob - inner_sum)).astype(jnp.bfloat16)
    grad_query = jnp.einsum("tu,ud->td", dscore, k_rot, preferred_element_type=f32) * score_scale
    grad_key = jnp.einsum("tu,td->ud", dscore, q_rot, preferred_element_type=f32) * score_scale
    grad_value = jnp.einsum("tu,td->ud", attention_bf, grad_context, preferred_element_type=f32)
    return (grad_query, grad_key, grad_value)


def swap(x):
    return lax.ppermute(x, ("xl", "core"), [(0, 0), (1, 2), (2, 1), (3, 3)])


def flip(x, axes):
    n = 2 ** len(axes)
    return lax.ppermute(x, axes, [(i, n - 1 - i) for i in range(n)])


def exchange(x, axes):
    return lax.all_to_all(x, axes, split_axis=0, concat_axis=0, tiled=True)


def spread(x, axes):
    n = lax.axis_size(axes)
    return exchange(jnp.broadcast_to(x[None], (n,) + x.shape), axes)


def ordered(mine, other, bit):
    first = jnp.where(bit == 0, mine, other)
    second = jnp.where(bit == 0, other, mine)
    return (first, second)


def local(hidden, cotangent, seg_ids, advantage, w_query, w_key, w_value):
    f32 = jnp.float32
    bf16 = jnp.bfloat16
    inv_width = D ** (-0.5)
    xh = lax.axis_index("xh")
    xl = lax.axis_index("xl")
    core = lax.axis_index("core")
    zl = lax.axis_index("zl")
    member = zl * 2 + core
    ring = xh * 2 + xl
    token_rows = hidden[0].astype(f32)
    normed_own = (
        token_rows * lax.rsqrt(jnp.mean(token_rows * token_rows, axis=-1, keepdims=True) + norm_eps)
    ).astype(bf16)
    normed_own = swap(normed_own)
    cot = swap(cotangent[0])
    seg_row = swap(seg_ids[0])
    adv_row = swap(advantage[0])
    normed = lax.all_gather(normed_own, YZ + ("core",), axis=0, tiled=True)
    block_len = normed.shape[0]
    wq = w_query.reshape(2, 64, 32, 2, HD)
    wq = lax.dynamic_index_in_dim(wq, xh, 0, keepdims=False)
    wq = lax.dynamic_index_in_dim(wq, core, 2, keepdims=False)
    wq = exchange(wq.transpose(1, 0, 2), YZ)
    wq_l = flip(wq, ("xl",))
    wq_h = flip(wq, ("xh",))
    wq_b = flip(wq, X)
    mine = ordered(wq, wq_l, xl)
    theirs = ordered(wq_h, wq_b, xl)
    row0 = ordered(mine[0], theirs[0], xh)
    row1 = ordered(mine[1], theirs[1], xh)
    q_cols = jnp.stack([row0[0], row0[1], row1[0], row1[1]], axis=1).reshape(D, HD)
    wkv = jnp.concatenate([w_key.reshape(128, 8, HD), w_value.reshape(128, 8, HD)], axis=-1)
    wkv = swap(exchange(wkv.transpose(1, 0, 2), KH))
    cosine_table, sine_table = angles(seg_row)
    weight_row = token_weights(seg_row, adv_row)
    grad_context = (cot.astype(f32) * weight_row[:, None]).astype(bf16)
    place = jnp.arange(block_len, dtype=jnp.int32)
    allowed = (seg_row[:, None] == seg_row[None, :]) & (place[None, :] <= place[:, None])
    normed_m = lax.dynamic_index_in_dim(
        normed.reshape(block_len, 8, 8, HD), member, 2, keepdims=False
    ).reshape(block_len, 1024)
    kv_part = jnp.dot(normed_m, wkv.reshape(1024, 2 * HD), preferred_element_type=f32)
    kv_own = jnp.sum(exchange(kv_part.reshape(8, 64, 2 * HD), MEM), axis=0) * inv_width
    cos_own = lax.dynamic_slice_in_dim(cosine_table, member * 64, 64)
    sin_own = lax.dynamic_slice_in_dim(sine_table, member * 64, 64)
    kv_own = jnp.concatenate([rotate(kv_own[:, :HD], cos_own, sin_own), kv_own[:, HD:]], -1).astype(
        bf16
    )
    kv = spread(kv_own, MEM).reshape(block_len, 2 * HD)
    queries = jnp.dot(normed, q_cols, preferred_element_type=f32) * inv_width
    q_rot = rotate(queries, cosine_table, sine_table).astype(bf16)
    grad_query, grad_key, grad_value = attend_back(
        q_rot, kv[:, :HD], kv[:, HD:], grad_context, allowed
    )
    scaled_q = (rotate(grad_query, cosine_table, -sine_table) * inv_width).astype(bf16)
    scaled_kv = (
        jnp.concatenate([rotate(grad_key, cosine_table, -sine_table), grad_value], -1) * inv_width
    ).astype(bf16)
    kv_sum = exchange(scaled_kv.reshape(8, 64, 2 * HD), MEM).astype(f32)
    kv_sum = jnp.sum(kv_sum, axis=0).astype(bf16)
    kv_sum = spread(kv_sum, MEM).reshape(block_len, 2 * HD)
    contract = (((0,), (0,)), ((), ()))
    part_q = lax.dot_general(normed, scaled_q, contract, preferred_element_type=f32).astype(bf16)
    part_q = exchange(part_q.reshape(4, 2048, HD), X).astype(f32)
    old_q = lax.dynamic_slice_in_dim(q_cols, ring * 2048, 2048)
    new_q = (old_q.astype(f32) - step_rate * jnp.sum(part_q, axis=0)).astype(bf16)
    near = swap(new_q)
    far = lax.ppermute(
        new_q,
        ("xh", "xl", "core"),
        [
            (h * 4 + l * 2 + c, (1 - h) * 4 + c * 2 + l)
            for h in (0, 1)
            for l in (0, 1)
            for c in (0, 1)
        ],
    )
    near_c = flip(near, ("core",))
    far_c = flip(far, ("core",))
    near = ordered(near, near_c, core)
    far = ordered(far, far_c, core)
    low = ordered(near[0], far[0], xh)
    high = ordered(near[1], far[1], xh)
    roll_q = jnp.stack([low[0], high[0], low[1], high[1]], axis=0).reshape(D, HD)
    part_kv = lax.dot_general(normed_m, kv_sum, contract, preferred_element_type=f32).astype(bf16)
    part_kv = exchange(part_kv.reshape(4, 256, 2 * HD), X).astype(f32)
    old_kv = lax.dynamic_slice_in_dim(wkv, ring * 2, 2).reshape(256, 2 * HD)
    new_kv = (old_kv.astype(f32) - step_rate * jnp.sum(part_kv, axis=0)).astype(bf16)
    new_kv = spread(new_kv, ("zl",))
    new_kv = spread(new_kv, X)
    other = flip(new_kv, ("core",))
    new_kv = jnp.stack(ordered(new_kv, other, core), axis=0)
    new_kv = new_kv.reshape(2, 4, 4, 2, 128, 2 * HD).transpose(1, 3, 2, 0, 4, 5).reshape(D, 2 * HD)
    return (roll_q, new_kv[:, :HD], new_kv[:, HD:])


def solution(mesh):
    grid = Mesh(mesh.devices.reshape(2, 4, 2, 4, 2, 2), ("xh", "y", "zh", "zl", "xl", "core"))
    groups = ("xh", "core")
    in_specs = (
        P(groups, FS, None),
        P(groups, None, FS),
        P(groups, None),
        P(groups, None),
        P(FS, None),
        P(FS, None),
        P(FS, None),
    )
    out_specs = (P(None, FS), P(None, FS), P(None, FS))
    return jax.shard_map(local, mesh=grid, in_specs=in_specs, out_specs=out_specs, check_vma=False)
```

profile of v0, /device:TPU:1, one launch (start us, length us, event | category | flops | bytes accessed | tf_op | source)
XLA Modules:
  0.0 324.4 jit_solution(6756234446904016995)
XLA Ops:
  9.4 4.5 %collective-permute-start.3 = (bf16[8,8192]{1,0:T(8,128)(2,1)S(1)}, bf16[8,8192]{1,0:T(8,128)(2,1)S(1)}, u32[]{:S(2)}, u32[]{:S(2)}) collective-permute-start(bf16[8,8192]{1,0:T(8,128)(2,1)S(1)} %fusion.11), channel_id=1, source_target_pairs={{0,0},{1,2},{2,1},{3,3},{4,4},{5,6},{6,5},{7,7},{8,8},{9,10},{10,9... | collective-permute-start | bytes 393224 | tf_op jit(solution)/shard_map/ppermute | solution.py:69
  23.1 11.3 %all-to-all-start = ((bf16[32,64,128]{2,1,0:T(8,128)(2,1)}), bf16[32,64,128]{2,1,0:T(8,128)(2,1)S(1)}, u32[]{:S(2)}, u32[]{:S(2)}) async-start(bf16[32,64,128]{2,1,0:T(8,128)(2,1)} %bitcast.87), calls=%async_computation | async-start | bytes 1048576 | tf_op jit(solution)/shard_map/all_to_all | solution.py:78
  35.4 14.5 %all-to-all-done = bf16[32,64,128]{2,1,0:T(8,128)(2,1)S(1)} async-done(((bf16[32,64,128]{2,1,0:T(8,128)(2,1)}), bf16[32,64,128]{2,1,0:T(8,128)(2,1)S(1)}, u32[]{:S(2)}, u32[]{:S(2)}) %all-to-all-start) | async-done | bytes 524320 | tf_op jit(solution)/shard_map/all_to_all | solution.py:78
  50.0 4.4 %all-to-all-start.1 = ((bf16[8,128,256]{2,1,0:T(8,128)(2,1)}), bf16[8,128,256]{2,1,0:T(8,128)(2,1)}, u32[]{:S(2)}, u32[]{:S(2)}) async-start(bf16[8,128,256]{2,1,0:T(8,128)(2,1)} %maximum_bitcast_fusion.1), calls=%async_computation.1 | async-start | bytes 1048576 | tf_op jit(solution)/shard_map/all_to_all | solution.py:78
  67.4 4.1 %all-to-all-done.1 = bf16[8,128,256]{2,1,0:T(8,128)(2,1)} async-done(((bf16[8,128,256]{2,1,0:T(8,128)(2,1)}), bf16[8,128,256]{2,1,0:T(8,128)(2,1)}, u32[]{:S(2)}, u32[]{:S(2)}) %all-to-all-start.1) | async-done | bytes 524320 | tf_op jit(solution)/shard_map/all_to_all | solution.py:78
  73.5 4.8 %collective-permute-start.5 = (bf16[8,128,256]{2,1,0:T(8,128)(2,1)}, bf16[8,128,256]{2,1,0:T(8,128)(2,1)S(1)}, u32[]{:S(2)}, u32[]{:S(2)}) collective-permute-start(bf16[8,128,256]{2,1,0:T(8,128)(2,1)} %all-to-all-done.1), channel_id=1, source_target_pairs={{0,0},{1,2},{2,1},{3,3},{4,4},{5,6},{6,5},{7,7},{8,8},{9,10},{10,9... | collective-permute-start | bytes 1572872 | tf_op jit(solution)/shard_map/ppermute | solution.py:69
  78.3 6.2 %collective-permute-done.1 = bf16[32,64,128]{2,1,0:T(8,128)(2,1)S(1)} collective-permute-done((bf16[32,64,128]{2,1,0:T(8,128)(2,1)S(1)}, bf16[32,64,128]{2,1,0:T(8,128)(2,1)S(1)}, u32[]{:S(2)}, u32[]{:S(2)}) %collective-permute-start.1) | collective-permute-done | bytes 524320 | tf_op jit(solution)/shard_map/ppermute | solution.py:74
  87.3 24.6 %all-gather.2.cloned.1.call-done = bf16[512,8192]{1,0:T(8,128)(2,1)} async-done(((bf16[8,8192]{1,0:T(8,128)(2,1)}), bf16[512,8192]{1,0:T(8,128)(2,1)}) %all-gather.2.cloned.1.call-update) | async-done | bytes 8388624 | tf_op jit(solution)/shard_map/all_gather | solution.py:110
  111.9 9.3 %copy.64 = bf16[64,8,64,128]{3,2,1,0:T(8,128)(2,1)} copy(bf16[64,8,64,128]{3,1,2,0:T(8,128)(2,1)} %bitcast.88) | data formatting | bytes 16777216
  121.2 5.6 %constant_dynamic-slice_fusion.1 = bf16[512,8,1,128]{3,2,1,0:T(2,128)(2,1)S(1)} fusion(bf16[512,8,8,128]{3,2,1,0:T(8,128)(2,1)} %bitcast.90, s32[]{:T(128)S(6)} %select_n.135), kind=kLoop, calls=%fused_computation.100 | loop fusion | bytes 2097156 | tf_op jit(solution)/shard_map/jit(dynamic_index_in_dim)/dynamic_slice | solution.py:131
  128.7 4.3 %all-to-all-start.2 = ((f32[8,64,256]{2,1,0:T(8,128)}), f32[8,64,256]{2,1,0:T(8,128)}, u32[]{:S(2)}, u32[]{:S(2)}) async-start(f32[8,64,256]{2,1,0:T(8,128)} %fusion.50), calls=%async_computation.2 | async-start | bytes 1048576 | tf_op jit(solution)/shard_map/all_to_all | solution.py:78
  134.8 6.3 %convolution_multiply_fusion.3 = f32[512,128]{0,1:T(8,128)S(1)} fusion(bf16[512,8192]{1,0:T(8,128)(2,1)} %all-gather.2.cloned.1.call-done, bf16[8192,128]{1,0:T(8,128)(2,1)S(1)} %bitcast.91), kind=kOutput, calls=%fused_computation.11 | convolution fusion | flops 1073807360 | bytes 10747904 | tf_op jit(solution)/shard_map/dot_general | solution.py:142
  142.3 5.2 %all-to-all-done.2 = f32[8,64,256]{2,1,0:T(8,128)} async-done(((f32[8,64,256]{2,1,0:T(8,128)}), f32[8,64,256]{2,1,0:T(8,128)}, u32[]{:S(2)}, u32[]{:S(2)}) %all-to-all-start.2) | async-done | bytes 524320 | tf_op jit(solution)/shard_map/all_to_all | solution.py:78
  150.4 4.3 %all-to-all-start.3 = ((bf16[8,64,256]{2,1,0:T(8,128)(2,1)}), bf16[8,64,256]{2,1,0:T(8,128)(2,1)S(1)}, u32[]{:S(2)}, u32[]{:S(2)}) async-start(bf16[8,64,256]{2,1,0:T(8,128)(2,1)} %broadcast_in_dim.11), calls=%async_computation.3 | async-start | bytes 524288 | tf_op jit(solution)/shard_map/all_to_all | solution.py:78
  156.0 7.4 %all-to-all-done.3 = bf16[8,64,256]{2,1,0:T(8,128)(2,1)S(1)} async-done(((bf16[8,64,256]{2,1,0:T(8,128)(2,1)}), bf16[8,64,256]{2,1,0:T(8,128)(2,1)S(1)}, u32[]{:S(2)}, u32[]{:S(2)}) %all-to-all-start.3) | async-done | bytes 262176 | tf_op jit(solution)/shard_map/all_to_all | solution.py:78
  173.2 12.1 %all_to_all.50 = bf16[8,64,256]{2,1,0:T(8,128)(2,1)S(1)} all-to-all(bf16[8,64,256]{2,1,0:T(8,128)(2,1)S(1)} %fusion.7), channel_id=1, replica_groups=mesh['xh'=2,'y'=4,'zh'=2,'zl'=4,'xl'=2,'core'=2] {'zl','core'}, dimensions={0} | all-to-all | bytes 524288 | tf_op jit(solution)/shard_map/all_to_all | solution.py:78
  186.7 12.1 %all_to_all.51 = bf16[8,64,256]{2,1,0:T(8,128)(2,1)S(1)} all-to-all(bf16[8,64,256]{2,1,0:T(8,128)(2,1)S(1)} %broadcast_in_dim.13), channel_id=1, replica_groups=mesh['xh'=2,'y'=4,'zh'=2,'zl'=4,'xl'=2,'core'=2] {'zl','core'}, dimensions={0} | all-to-all | bytes 524288 | tf_op jit(solution)/shard_map/all_to_all | solution.py:78
  204.1 7.1 %convolution_convert_fusion = bf16[8192,128]{1,0:T(8,128)(2,1)} fusion(bf16[512,8192]{1,0:T(8,128)(2,1)} %all-gather.2.cloned.1.call-done, f32[512,64]{0,1:T(8,128)S(1)} %get-tuple-element.23, f32[512,64]{0,1:T(8,128)S(1)} %copy-done.7), kind=kOutput, calls=%fused_computation | convolution fusion | flops 1074987008 | bytes 10747904 | tf_op jit(solution)/shard_map/dot_general | solution.py:155
  212.1 4.5 %all-to-all-start.4 = ((bf16[4,2048,128]{2,1,0:T(8,128)(2,1)}), bf16[4,2048,128]{2,1,0:T(8,128)(2,1)}, u32[]{:S(2)}, u32[]{:S(2)}) async-start(bf16[4,2048,128]{2,1,0:T(8,128)(2,1)} %bitcast.18), calls=%async_computation.4 | async-start | bytes 4194304 | tf_op jit(solution)/shard_map/all_to_all | solution.py:78
  217.6 23.0 %all-to-all-done.4 = bf16[4,2048,128]{2,1,0:T(8,128)(2,1)} async-done(((bf16[4,2048,128]{2,1,0:T(8,128)(2,1)}), bf16[4,2048,128]{2,1,0:T(8,128)(2,1)}, u32[]{:S(2)}, u32[]{:S(2)}) %all-to-all-start.4) | async-done | bytes 2097184 | tf_op jit(solution)/shard_map/all_to_all | solution.py:78
  240.6 17.9 %all_to_all.52 = bf16[4,256,256]{2,1,0:T(8,128)(2,1)S(1)} all-to-all(bf16[4,256,256]{2,1,0:T(8,128)(2,1)S(1)} %broadcast_in_dim.14), channel_id=1, replica_groups=mesh['xh'=2,'y'=4,'zh'=2,'zl'=4,'xl'=2,'core'=2] {'zl'}, dimensions={0} | all-to-all | bytes 1048576 | tf_op jit(solution)/shard_map/all_to_all | solution.py:78
  260.0 4.4 %all-to-all-start.9 = ((bf16[4,4,256,256]{3,2,1,0:T(8,128)(2,1)}), bf16[4,4,256,256]{3,2,1,0:T(8,128)(2,1)}, u32[]{:S(2)}, u32[]{:S(2)}) async-start(bf16[4,4,256,256]{3,2,1,0:T(8,128)(2,1)} %broadcast_in_dim.15), calls=%async_computation.9 | async-start | bytes 4194304 | tf_op jit(solution)/shard_map/all_to_all | solution.py:78
  266.5 22.5 %all-to-all-done.9 = bf16[4,4,256,256]{3,2,1,0:T(8,128)(2,1)} async-done(((bf16[4,4,256,256]{3,2,1,0:T(8,128)(2,1)}), bf16[4,4,256,256]{3,2,1,0:T(8,128)(2,1)}, u32[]{:S(2)}, u32[]{:S(2)}) %all-to-all-start.9) | async-done | bytes 2097184 | tf_op jit(solution)/shard_map/all_to_all | solution.py:78
  295.0 12.5 %collective-permute-done.10 = bf16[2048,128]{1,0:T(8,128)(2,1)S(1)} collective-permute-done((bf16[2048,128]{1,0:T(8,128)(2,1)S(1)}, bf16[2048,128]{1,0:T(8,128)(2,1)S(1)}, u32[]{:S(2)}, u32[]{:S(2)}) %collective-permute-start.10) | collective-permute-done | bytes 524320 | tf_op jit(solution)/shard_map/ppermute | solution.py:160
  (110 shorter events, 77.1 us)
Async XLA Ops:
  7.2 27.3 %copy-start = (bf16[128,1024]{1,0:T(8,128)(2,1)S(1)}, bf16[128,1024]{1,0:T(8,128)(2,1)}, u32[]{:S(2)}) copy-start(bf16[128,1024]{1,0:T(8,128)(2,1)} %param.12) | copy-start | bytes 786436
  7.2 104.7 %all-gather.2.cloned.1.call-start = ((), (), s32[]{:S(2)}) async-start(), calls=%async_computation.10 | async-start | bytes 8519680 | tf_op jit(solution)/shard_map/all_gather | solution.py:110
  9.4 7.1 %collective-permute-start.3 = (bf16[8,8192]{1,0:T(8,128)(2,1)S(1)}, bf16[8,8192]{1,0:T(8,128)(2,1)S(1)}, u32[]{:S(2)}, u32[]{:S(2)}) collective-permute-start(bf16[8,8192]{1,0:T(8,128)(2,1)S(1)} %fusion.11), channel_id=1, source_target_pairs={{0,0},{1,2},{2,1},{3,3},{4,4},{5,6},{6,5},{7,7},{8,8},{9,10},{10,9... | collective-permute-start | bytes 393224 | tf_op jit(solution)/shard_map/ppermute | solution.py:69
  23.1 31.3 %copy-start.13 = (s32[1,512]{1,0:T(1,128)S(1)}, s32[1,512]{1,0:T(1,128)}, u32[]{:S(2)}) copy-start(s32[1,512]{1,0:T(1,128)} %param.9) | copy-start | bytes 6148
  23.1 26.9 %all-to-all-start = ((bf16[32,64,128]{2,1,0:T(8,128)(2,1)}), bf16[32,64,128]{2,1,0:T(8,128)(2,1)S(1)}, u32[]{:S(2)}, u32[]{:S(2)}) async-start(bf16[32,64,128]{2,1,0:T(8,128)(2,1)} %bitcast.87), calls=%async_computation | async-start | bytes 1048576 | tf_op jit(solution)/shard_map/all_to_all | solution.py:78
  50.0 21.5 %all-to-all-start.1 = ((bf16[8,128,256]{2,1,0:T(8,128)(2,1)}), bf16[8,128,256]{2,1,0:T(8,128)(2,1)}, u32[]{:S(2)}, u32[]{:S(2)}) async-start(bf16[8,128,256]{2,1,0:T(8,128)(2,1)} %maximum_bitcast_fusion.1), calls=%async_computation.1 | async-start | bytes 1048576 | tf_op jit(solution)/shard_map/all_to_all | solution.py:78
  54.4 9.6 %collective-permute-start.4 = (s32[512]{0:T(512)S(1)}, s32[512]{0:T(512)S(1)}, u32[]{:S(2)}, u32[]{:S(2)}) collective-permute-start(s32[512]{0:T(512)S(1)} %bitcast.106), channel_id=1, source_target_pairs={{0,0},{1,2},{2,1},{3,3},{4,4},{5,6},{6,5},{7,7},{8,8},{9,10},{10,9... | collective-permute-start | bytes 6152 | tf_op jit(solution)/shard_map/ppermute | solution.py:69
  57.9 96.8 %collective-permute-start.7 = (f32[8]{0:T(128)}, f32[8]{0:T(128)}, u32[]{:S(2)}, u32[]{:S(2)}) collective-permute-start(f32[8]{0:T(128)} %bitcast.17), channel_id=1, source_target_pairs={{0,0},{1,2},{2,1},{3,3},{4,4},{5,6},{6,5},{7,7},{8,8},{9,10},{10,9... | collective-permute-start | bytes 104 | tf_op jit(solution)/shard_map/ppermute | solution.py:69
  59.9 13.6 %collective-permute-start = (bf16[32,64,128]{2,1,0:T(8,128)(2,1)S(1)}, bf16[32,64,128]{2,1,0:T(8,128)(2,1)S(1)}, u32[]{:S(2)}, u32[]{:S(2)}) collective-permute-start(bf16[32,64,128]{2,1,0:T(8,128)(2,1)S(1)} %all-to-all-done), channel_id=1, source_target_pairs={{0,2},{2,0},{1,3},{3,1},{4,6},{6,4},{5,7},{7,5},{8,10},{10,8},{9,1... | collective-permute-start | bytes 1572872 | tf_op jit(solution)/shard_map/ppermute | solution.py:74
  60.0 24.5 %collective-permute-start.1 = (bf16[32,64,128]{2,1,0:T(8,128)(2,1)S(1)}, bf16[32,64,128]{2,1,0:T(8,128)(2,1)S(1)}, u32[]{:S(2)}, u32[]{:S(2)}) collective-permute-start(bf16[32,64,128]{2,1,0:T(8,128)(2,1)S(1)} %all-to-all-done), channel_id=1, source_target_pairs={{0,128},{128,0},{1,129},{129,1},{2,130},{130,2},{3,131},{131,3},{4... | collective-permute-start | bytes 1572872 | tf_op jit(solution)/shard_map/ppermute | solution.py:74
  62.8 22.9 %collective-permute-start.2 = (bf16[32,64,128]{2,1,0:T(8,128)(2,1)S(1)}, bf16[32,64,128]{2,1,0:T(8,128)(2,1)S(1)}, u32[]{:S(2)}, u32[]{:S(2)}) collective-permute-start(bf16[32,64,128]{2,1,0:T(8,128)(2,1)S(1)} %all-to-all-done), channel_id=1, source_target_pairs={{0,130},{2,128},{128,2},{130,0},{1,131},{3,129},{129,3},{131,1},{4... | collective-permute-start | bytes 1572872 | tf_op jit(solution)/shard_map/ppermute | solution.py:74
  63.9 77.2 %copy-start.11 = (f32[64]{0:T(128)}, f32[64]{0:T(128)S(1)}, u32[]{:S(2)}) copy-start(f32[64]{0:T(128)S(1)} %multiply_power_fusion) | copy-start | bytes 772
  63.9 100.1 %collective-permute-start.6 = (bf16[512,128]{1,0:T(8,128)(2,1)}, bf16[512,128]{1,0:T(8,128)(2,1)}, u32[]{:S(2)}, u32[]{:S(2)}) collective-permute-start(bf16[512,128]{1,0:T(8,128)(2,1)} %bitcast.16), channel_id=1, source_target_pairs={{0,0},{1,2},{2,1},{3,3},{4,4},{5,6},{6,5},{7,7},{8,8},{9,10},{10,9... | collective-permute-start | bytes 393224 | tf_op jit(solution)/shard_map/ppermute | solution.py:69
  73.5 53.9 %collective-permute-start.5 = (bf16[8,128,256]{2,1,0:T(8,128)(2,1)}, bf16[8,128,256]{2,1,0:T(8,128)(2,1)S(1)}, u32[]{:S(2)}, u32[]{:S(2)}) collective-permute-start(bf16[8,128,256]{2,1,0:T(8,128)(2,1)} %all-to-all-done.1), channel_id=1, source_target_pairs={{0,0},{1,2},{2,1},{3,3},{4,4},{5,6},{6,5},{7,7},{8,8},{9,10},{10,9... | collective-permute-start | bytes 1572872 | tf_op jit(solution)/shard_map/ppermute | solution.py:69
  128.7 18.8 %all-to-all-start.2 = ((f32[8,64,256]{2,1,0:T(8,128)}), f32[8,64,256]{2,1,0:T(8,128)}, u32[]{:S(2)}, u32[]{:S(2)}) async-start(f32[8,64,256]{2,1,0:T(8,128)} %fusion.50), calls=%async_computation.2 | async-start | bytes 1048576 | tf_op jit(solution)/shard_map/all_to_all | solution.py:78
  150.4 13.0 %all-to-all-start.3 = ((bf16[8,64,256]{2,1,0:T(8,128)(2,1)}), bf16[8,64,256]{2,1,0:T(8,128)(2,1)S(1)}, u32[]{:S(2)}, u32[]{:S(2)}) async-start(bf16[8,64,256]{2,1,0:T(8,128)(2,1)} %broadcast_in_dim.11), calls=%async_computation.3 | async-start | bytes 524288 | tf_op jit(solution)/shard_map/all_to_all | solution.py:78
  200.2 11.9 %all-to-all-start.7 = ((bf16[4,256,256]{2,1,0:T(8,128)(2,1)}), bf16[4,256,256]{2,1,0:T(8,128)(2,1)S(1)}, u32[]{:S(2)}, u32[]{:S(2)}) async-start(bf16[4,256,256]{2,1,0:T(8,128)(2,1)} %bitcast.103), calls=%async_computation.7 | async-start | bytes 1048576 | tf_op jit(solution)/shard_map/all_to_all | solution.py:78
  212.1 28.5 %all-to-all-start.4 = ((bf16[4,2048,128]{2,1,0:T(8,128)(2,1)}), bf16[4,2048,128]{2,1,0:T(8,128)(2,1)}, u32[]{:S(2)}, u32[]{:S(2)}) async-start(bf16[4,2048,128]{2,1,0:T(8,128)(2,1)} %bitcast.18), calls=%async_computation.4 | async-start | bytes 4194304 | tf_op jit(solution)/shard_map/all_to_all | solution.py:78
  260.0 28.9 %all-to-all-start.9 = ((bf16[4,4,256,256]{3,2,1,0:T(8,128)(2,1)}), bf16[4,4,256,256]{3,2,1,0:T(8,128)(2,1)}, u32[]{:S(2)}, u32[]{:S(2)}) async-start(bf16[4,4,256,256]{3,2,1,0:T(8,128)(2,1)} %broadcast_in_dim.15), calls=%async_computation.9 | async-start | bytes 4194304 | tf_op jit(solution)/shard_map/all_to_all | solution.py:78
  289.0 22.9 %collective-permute-start.12 = (bf16[4,4,256,256]{3,2,1,0:T(8,128)(2,1)}, bf16[4,4,256,256]{3,2,1,0:T(8,128)(2,1)}, u32[]{:S(2)}, u32[]{:S(2)}) collective-permute-start(bf16[4,4,256,256]{3,2,1,0:T(8,128)(2,1)} %all-to-all-done.9), channel_id=1, source_target_pairs={{0,1},{1,0},{2,3},{3,2},{4,5},{5,4},{6,7},{7,6},{8,9},{9,8},{10,11... | collective-permute-start | bytes 6291464 | tf_op jit(solution)/shard_map/ppermute | solution.py:74
  292.0 15.5 %collective-permute-start.10 = (bf16[2048,128]{1,0:T(8,128)(2,1)S(1)}, bf16[2048,128]{1,0:T(8,128)(2,1)S(1)}, u32[]{:S(2)}, u32[]{:S(2)}) collective-permute-start(bf16[2048,128]{1,0:T(8,128)(2,1)S(1)} %subtract_convert_fusion), channel_id=1, source_target_pairs={{0,128},{1,130},{2,129},{3,131},{128,0},{129,2},{130,1},{131,3},{4... | collective-permute-start | bytes 1572872 | tf_op jit(solution)/shard_map/ppermute | solution.py:160
  292.8 14.7 %collective-permute-start.8 = (bf16[2048,128]{1,0:T(8,128)(2,1)S(1)}, bf16[2048,128]{1,0:T(8,128)(2,1)S(1)}, u32[]{:S(2)}, u32[]{:S(2)}) collective-permute-start(bf16[2048,128]{1,0:T(8,128)(2,1)S(1)} %subtract_convert_fusion), channel_id=1, source_target_pairs={{0,0},{1,2},{2,1},{3,3},{4,4},{5,6},{6,5},{7,7},{8,8},{9,10},{10,9... | collective-permute-start | bytes 1572872 | tf_op jit(solution)/shard_map/ppermute | solution.py:69
  307.5 1.9 collective-permute-start.11
  307.5 2.7 collective-permute-start.9
  (11 other events, 36.6 us)
Sparse Core Ops, SparseCore 0:
  17.3 94.5 all-gather.1
where the time goes:
time: 326 us; the launch traced here: 324 us
  waiting for transfers between devices  129 us (40%)
  starting transfers between devices  65.5 us (20%)
  blocking collectives  42.1 us (13%)
  local copies, waits for them, and re-layouts  32.5 us (10%)
  other arithmetic  20.9 us (6%)
  matrix products  20 us (6%)
  between operations  14.5 us (4%)
    all_to_all x7, waiting for transfers between devices, exchange(): return lax.all_to_all(x, axes, split_axis=0, concat_axis=0, tiled=True)  77.5 us
    all_to_all x3, blocking collectives, exchange(): return lax.all_to_all(x, axes, split_axis=0, concat_axis=0, tiled=True)  42.1 us
    all_to_all x7, starting transfers between devices, exchange(): return lax.all_to_all(x, axes, split_axis=0, concat_axis=0, tiled=True)  37.2 us
    all_gather x1, waiting for transfers between devices, local(): normed = lax.all_gather(normed_own, YZ + ('core',), axis=0, tiled=True)  24.6 us
    ppermute x6, starting transfers between devices, swap(): return lax.ppermute(x, ('xl', 'core'), [(0, 0), (1, 2), (2, 1), (3, 3)])  20.1 us
    ppermute x1, waiting for transfers between devices, local(): lax.ppermute(new_q, ('xh', 'xl', 'core'), [(h * 4 + l * 2 + c, (1 - h) *...  12.5 us
    ppermute x6, waiting for transfers between devices, flip(): return lax.ppermute(x, axes, [(i, n - 1 - i) for i in range(n)])  11.6 us
    unnamed x30, local copies, waits for them, and re-layouts  10.7 us
  transfers between devices with their start and end apart: 21, of which 15 were waited for; matrix products, arithmetic and copies ran while one was open for 16% of the time, Pallas kernels for 0%

commit v1 on v0

--- a/solution.py
+++ b/solution.py
@@ -107,7 +107,12 @@
     cot = swap(cotangent[0])
     seg_row = swap(seg_ids[0])
     adv_row = swap(advantage[0])
-    normed = lax.all_gather(normed_own, YZ + ("core",), axis=0, tiled=True)
+    normed = jnp.concatenate(
+        lax.all_to_all(
+            jnp.stack([normed_own] * lax.axis_size(YZ + ("core",))), YZ + ("core",), 0, 0
+        ),
+        axis=0,
+    )
     block_len = normed.shape[0]
     wq = w_query.reshape(2, 64, 32, 2, HD)
     wq = lax.dynamic_index_in_dim(wq, xh, 0, keepdims=False)

time: 326 us -> 460 us (1.41)
  waiting for transfers between devices: 129 us -> 261 us
  starting transfers between devices: 65.5 us -> 83.9 us
  local copies, waits for them, and re-layouts: 32.5 us -> 47.1 us
  between operations: 14.5 us -> 1.1 us
  blocking collectives: 42.1 us -> 30 us
  other arithmetic: 20.9 us -> 15.7 us
    all_to_all x0 -> x1, waiting for transfers between devices: none -> 153 us  [local(): lax.all_to_all(jnp.stack([normed_own] * lax.axis_size(YZ + ('core',))), Y...]
    all_gather x1 -> x0, waiting for transfers between devices: 24.6 us -> none  [local(): normed = lax.all_gather(normed_own, YZ + ('core',), axis=0, tiled=True)]
    all_to_all x3 -> x2, blocking collectives: 42.1 us -> 30 us  [exchange(): return lax.all_to_all(x, axes, split_axis=0, concat_axis=0, tiled=True)]
    all_to_all x0 -> x1, starting transfers between devices: none -> 10.2 us  [local(): lax.all_to_all(jnp.stack([normed_own] * lax.axis_size(YZ + ('core',))), Y...]
    dynamic_slice x1 -> x2, local copies, waits for them, and re-layouts: 5.59 us -> 14.9 us  [local(): lax.dynamic_index_in_dim(normed.reshape(block_len, 8, 8, HD), member, 2,...]
    all_to_all x7 -> x8, starting transfers between devices: 37.2 us -> 45 us  [exchange(): return lax.all_to_all(x, axes, split_axis=0, concat_axis=0, tiled=True)]
    all_to_all x7 -> x8, waiting for transfers between devices: 77.5 us -> 77.3 us  [exchange(): return lax.all_to_all(x, axes, split_axis=0, concat_axis=0, tiled=True)]
    unnamed x30 -> x23, local copies, waits for them, and re-layouts: 10.7 us -> 10.9 us
  transfers between devices with their start and end apart: 21 -> 22, of which waited for: 15 -> 16; matrix products, arithmetic and copies ran while one was open for 16% -> 13% of each run, Pallas kernels for 0% -> 0%
where the time goes in v1:
time: 460 us; the launch traced here: 458 us
  waiting for transfers between devices  261 us (57%)
  starting transfers between devices  83.9 us (18%)
  local copies, waits for them, and re-layouts  47.1 us (10%)
  blocking collectives  30 us (7%)
  matrix products  19.6 us (4%)
  other arithmetic  15.7 us (3%)
    all_to_all x1, waiting for transfers between devices, local(): lax.all_to_all(jnp.stack([normed_own] * lax.axis_size(YZ + ('core',))), Y...  153 us
    all_to_all x8, waiting for transfers between devices, exchange(): return lax.all_to_all(x, axes, split_axis=0, concat_axis=0, tiled=True)  77.3 us
    all_to_all x8, starting transfers between devices, exchange(): return lax.all_to_all(x, axes, split_axis=0, concat_axis=0, tiled=True)  45 us
    all_to_all x2, blocking collectives, exchange(): return lax.all_to_all(x, axes, split_axis=0, concat_axis=0, tiled=True)  30 us
    ppermute x6, starting transfers between devices, swap(): return lax.ppermute(x, ('xl', 'core'), [(0, 0), (1, 2), (2, 1), (3, 3)])  20.5 us
    ppermute x6, waiting for transfers between devices, flip(): return lax.ppermute(x, axes, [(i, n - 1 - i) for i in range(n)])  15.5 us
    dynamic_slice x2, local copies, waits for them, and re-layouts, local(): lax.dynamic_index_in_dim(normed.reshape(block_len, 8, 8, HD), member, 2,...  14.9 us
    ppermute x1, waiting for transfers between devices, local(): lax.ppermute(new_q, ('xh', 'xl', 'core'), [(h * 4 + l * 2 + c, (1 - h) *...  12.5 us
  transfers between devices with their start and end apart: 22, of which 16 were waited for; matrix products, arithmetic and copies ran while one was open for 13% of the time, Pallas kernels for 0%

profile of v1, /device:TPU:1, one launch (start us, length us, event | category | flops | bytes accessed | tf_op | source)
XLA Modules:
  0.0 458.4 jit_solution(11540778766408248653)
XLA Ops:
  3.5 11.6 %all-to-all-start.2 = ((bf16[8,128,256]{2,1,0:T(8,128)(2,1)}), bf16[8,128,256]{2,1,0:T(8,128)(2,1)}, u32[]{:S(2)}, u32[]{:S(2)}) async-start(bf16[8,128,256]{2,1,0:T(8,128)(2,1)} %maximum_bitcast_fusion.1), calls=%async_computation.2 | async-start | bytes 1048576 | tf_op jit(solution)/shard_map/all_to_all | solution.py:78
  21.2 8.2 %all-to-all-done.2 = bf16[8,128,256]{2,1,0:T(8,128)(2,1)} async-done(((bf16[8,128,256]{2,1,0:T(8,128)(2,1)}), bf16[8,128,256]{2,1,0:T(8,128)(2,1)}, u32[]{:S(2)}, u32[]{:S(2)}) %all-to-all-start.2) | async-done | bytes 524320 | tf_op jit(solution)/shard_map/all_to_all | solution.py:78
  29.4 8.2 %all-to-all-start = ((bf16[32,64,128]{2,1,0:T(8,128)(2,1)}), bf16[32,64,128]{2,1,0:T(8,128)(2,1)S(1)}, u32[]{:S(2)}, u32[]{:S(2)}) async-start(bf16[32,64,128]{2,1,0:T(8,128)(2,1)} %bitcast.85), calls=%async_computation | async-start | bytes 1048576 | tf_op jit(solution)/shard_map/all_to_all | solution.py:78
  37.7 4.7 %collective-permute-start.3 = (bf16[8,8192]{1,0:T(8,128)(2,1)S(1)}, bf16[8,8192]{1,0:T(8,128)(2,1)S(1)}, u32[]{:S(2)}, u32[]{:S(2)}) collective-permute-start(bf16[8,8192]{1,0:T(8,128)(2,1)S(1)} %fusion.15), channel_id=1, source_target_pairs={{0,0},{1,2},{2,1},{3,3},{4,4},{5,6},{6,5},{7,7},{8,8},{9,10},{10,9... | collective-permute-start | bytes 393224 | tf_op jit(solution)/shard_map/ppermute | solution.py:69
  45.3 6.0 %all-to-all-done = bf16[32,64,128]{2,1,0:T(8,128)(2,1)S(1)} async-done(((bf16[32,64,128]{2,1,0:T(8,128)(2,1)}), bf16[32,64,128]{2,1,0:T(8,128)(2,1)S(1)}, u32[]{:S(2)}, u32[]{:S(2)}) %all-to-all-start) | async-done | bytes 524320 | tf_op jit(solution)/shard_map/all_to_all | solution.py:78
  55.6 10.2 %all-to-all-start.1 = ((bf16[64,8,8192]{2,1,0:T(8,128)(2,1)}), bf16[64,8,8192]{2,1,0:T(8,128)(2,1)}, u32[]{:S(2)}, u32[]{:S(2)}) async-start(bf16[64,8,8192]{2,1,0:T(8,128)(2,1)} %stack.33), calls=%async_computation.1 | async-start | bytes 16777216 | tf_op jit(solution)/shard_map/all_to_all | solution.py:111
  78.9 6.2 %collective-permute-done = bf16[32,64,128]{2,1,0:T(8,128)(2,1)S(1)} collective-permute-done((bf16[32,64,128]{2,1,0:T(8,128)(2,1)S(1)}, bf16[32,64,128]{2,1,0:T(8,128)(2,1)S(1)}, u32[]{:S(2)}, u32[]{:S(2)}) %collective-permute-start) | collective-permute-done | bytes 524320 | tf_op jit(solution)/shard_map/ppermute | solution.py:74
  85.0 4.9 %collective-permute-start.5 = (bf16[8,128,256]{2,1,0:T(8,128)(2,1)}, bf16[8,128,256]{2,1,0:T(8,128)(2,1)S(1)}, u32[]{:S(2)}, u32[]{:S(2)}) collective-permute-start(bf16[8,128,256]{2,1,0:T(8,128)(2,1)} %all-to-all-done.2), channel_id=1, source_target_pairs={{0,0},{1,2},{2,1},{3,3},{4,4},{5,6},{6,5},{7,7},{8,8},{9,10},{10,9... | collective-permute-start | bytes 1572872 | tf_op jit(solution)/shard_map/ppermute | solution.py:69
  90.0 6.3 %collective-permute-done.1 = bf16[32,64,128]{2,1,0:T(8,128)(2,1)S(1)} collective-permute-done((bf16[32,64,128]{2,1,0:T(8,128)(2,1)S(1)}, bf16[32,64,128]{2,1,0:T(8,128)(2,1)S(1)}, u32[]{:S(2)}, u32[]{:S(2)}) %collective-permute-start.1) | collective-permute-done | bytes 524320 | tf_op jit(solution)/shard_map/ppermute | solution.py:74
  98.6 152.9 %all-to-all-done.1 = bf16[64,8,8192]{2,1,0:T(8,128)(2,1)} async-done(((bf16[64,8,8192]{2,1,0:T(8,128)(2,1)}), bf16[64,8,8192]{2,1,0:T(8,128)(2,1)}, u32[]{:S(2)}, u32[]{:S(2)}) %all-to-all-start.1) | async-done | bytes 8388640 | tf_op jit(solution)/shard_map/all_to_all | solution.py:111
  251.5 9.3 %copy.61 = bf16[64,8,64,128]{3,2,1,0:T(8,128)(2,1)} copy(bf16[64,8,64,128]{3,1,2,0:T(8,128)(2,1)} %bitcast.49) | data formatting | bytes 16777216
  260.9 10.3 %fusion.53 = (bf16[512,8,128]{2,1,0:T(8,128)(2,1)S(1)}, bf16[512,8,1,128]{3,2,1,0:T(2,128)(2,1)}) fusion(bf16[512,8,8,128]{3,2,1,0:T(8,128)(2,1)} %bitcast.87, s32[]{:T(128)S(6)} %select_n.135), kind=kLoop, calls=%fused_computation.110 | loop fusion | bytes 3145732 | tf_op jit(solution)/shard_map/jit(dynamic_index_in_dim)/dynamic_slice | solution.py:136
  278.3 6.3 %fusion.3 = f32[512,128]{0,1:T(8,128)S(1)} fusion(bf16[8192,128]{1,0:T(8,128)(2,1)S(1)} %bitcast.88, bf16[64,8,8192]{2,1,0:T(8,128)(2,1)} %all-to-all-done.1), kind=kOutput, calls=%fused_computation.14 | convolution fusion | flops 1073807360 | bytes 10747904 | tf_op jit(solution)/shard_map/dot_general | solution.py:147
  285.1 5.2 %all-to-all-done.3 = f32[8,64,256]{2,1,0:T(8,128)S(1)} async-done(((f32[8,64,256]{2,1,0:T(8,128)}), f32[8,64,256]{2,1,0:T(8,128)S(1)}, u32[]{:S(2)}, u32[]{:S(2)}) %all-to-all-start.3) | async-done | bytes 524320 | tf_op jit(solution)/shard_map/all_to_all | solution.py:78
  297.0 7.4 %all-to-all-done.4 = bf16[8,64,256]{2,1,0:T(8,128)(2,1)S(1)} async-done(((bf16[8,64,256]{2,1,0:T(8,128)(2,1)}), bf16[8,64,256]{2,1,0:T(8,128)(2,1)S(1)}, u32[]{:S(2)}, u32[]{:S(2)}) %all-to-all-start.4) | async-done | bytes 262176 | tf_op jit(solution)/shard_map/all_to_all | solution.py:78
  313.8 12.1 %all_to_all.55 = bf16[8,64,256]{2,1,0:T(8,128)(2,1)S(1)} all-to-all(bf16[8,64,256]{2,1,0:T(8,128)(2,1)S(1)} %fusion.11), channel_id=1, replica_groups=mesh['xh'=2,'y'=4,'zh'=2,'zl'=4,'xl'=2,'core'=2] {'zl','core'}, dimensions={0} | all-to-all | bytes 524288 | tf_op jit(solution)/shard_map/all_to_all | solution.py:78
  331.0 4.6 copy.51
  345.0 7.1 %convolution_convert_fusion = bf16[8192,128]{1,0:T(8,128)(2,1)} fusion(bf16[64,8,8192]{2,1,0:T(8,128)(2,1)} %all-to-all-done.1, f32[512,64]{0,1:T(8,128)S(1)} %get-tuple-element.25, f32[512,64]{0,1:T(8,128)} %get-tuple-element.26), kind=kOutput, calls=%fused_computation | convolution fusion | flops 1074987008 | bytes 10747904 | tf_op jit(solution)/shard_map/dot_general | solution.py:160
  352.9 4.4 all-to-all-start.5
  358.4 23.0 %all-to-all-done.5 = bf16[4,2048,128]{2,1,0:T(8,128)(2,1)} async-done(((bf16[4,2048,128]{2,1,0:T(8,128)(2,1)}), bf16[4,2048,128]{2,1,0:T(8,128)(2,1)}, u32[]{:S(2)}, u32[]{:S(2)}) %all-to-all-start.5) | async-done | bytes 2097184 | tf_op jit(solution)/shard_map/all_to_all | solution.py:78
  381.4 17.8 %all_to_all.56 = bf16[4,256,256]{2,1,0:T(8,128)(2,1)S(1)} all-to-all(bf16[4,256,256]{2,1,0:T(8,128)(2,1)S(1)} %broadcast_in_dim.14), channel_id=1, replica_groups=mesh['xh'=2,'y'=4,'zh'=2,'zl'=4,'xl'=2,'core'=2] {'zl'}, dimensions={0} | all-to-all | bytes 1048576 | tf_op jit(solution)/shard_map/all_to_all | solution.py:78
  400.8 4.5 all-to-all-start.10
  407.3 22.5 %all-to-all-done.10 = bf16[4,4,256,256]{3,2,1,0:T(8,128)(2,1)} async-done(((bf16[4,4,256,256]{3,2,1,0:T(8,128)(2,1)}), bf16[4,4,256,256]{3,2,1,0:T(8,128)(2,1)}, u32[]{:S(2)}, u32[]{:S(2)}) %all-to-all-start.10) | async-done | bytes 2097184 | tf_op jit(solution)/shard_map/all_to_all | solution.py:78
  435.8 12.5 %collective-permute-done.10 = bf16[2048,128]{1,0:T(8,128)(2,1)S(1)} collective-permute-done((bf16[2048,128]{1,0:T(8,128)(2,1)S(1)}, bf16[2048,128]{1,0:T(8,128)(2,1)S(1)}, u32[]{:S(2)}, u32[]{:S(2)}) %collective-permute-start.10) | collective-permute-done | bytes 524320 | tf_op jit(solution)/shard_map/ppermute | solution.py:165
  (105 shorter events, 91.2 us)
Async XLA Ops:
  3.5 25.9 %all-to-all-start.2 = ((bf16[8,128,256]{2,1,0:T(8,128)(2,1)}), bf16[8,128,256]{2,1,0:T(8,128)(2,1)}, u32[]{:S(2)}, u32[]{:S(2)}) async-start(bf16[8,128,256]{2,1,0:T(8,128)(2,1)} %maximum_bitcast_fusion.1), calls=%async_computation.2 | async-start | bytes 1048576 | tf_op jit(solution)/shard_map/all_to_all | solution.py:78
  29.4 21.9 %all-to-all-start = ((bf16[32,64,128]{2,1,0:T(8,128)(2,1)}), bf16[32,64,128]{2,1,0:T(8,128)(2,1)S(1)}, u32[]{:S(2)}, u32[]{:S(2)}) async-start(bf16[32,64,128]{2,1,0:T(8,128)(2,1)} %bitcast.85), calls=%async_computation | async-start | bytes 1048576 | tf_op jit(solution)/shard_map/all_to_all | solution.py:78
  37.7 7.6 %collective-permute-start.3 = (bf16[8,8192]{1,0:T(8,128)(2,1)S(1)}, bf16[8,8192]{1,0:T(8,128)(2,1)S(1)}, u32[]{:S(2)}, u32[]{:S(2)}) collective-permute-start(bf16[8,8192]{1,0:T(8,128)(2,1)S(1)} %fusion.15), channel_id=1, source_target_pairs={{0,0},{1,2},{2,1},{3,3},{4,4},{5,6},{6,5},{7,7},{8,8},{9,10},{10,9... | collective-permute-start | bytes 393224 | tf_op jit(solution)/shard_map/ppermute | solution.py:69
  55.6 10.2 %copy-start.10 = (s32[1,512]{1,0:T(1,128)S(1)}, s32[1,512]{1,0:T(1,128)}, u32[]{:S(2)}) copy-start(s32[1,512]{1,0:T(1,128)} %param.9) | copy-start | bytes 6148
  55.6 195.9 %all-to-all-start.1 = ((bf16[64,8,8192]{2,1,0:T(8,128)(2,1)}), bf16[64,8,8192]{2,1,0:T(8,128)(2,1)}, u32[]{:S(2)}, u32[]{:S(2)}) async-start(bf16[64,8,8192]{2,1,0:T(8,128)(2,1)} %stack.33), calls=%async_computation.1 | async-start | bytes 16777216 | tf_op jit(solution)/shard_map/all_to_all | solution.py:111
  65.8 9.6 %collective-permute-start.4 = (s32[512]{0:T(512)S(1)}, s32[512]{0:T(512)S(1)}, u32[]{:S(2)}, u32[]{:S(2)}) collective-permute-start(s32[512]{0:T(512)S(1)} %bitcast.103), channel_id=1, source_target_pairs={{0,0},{1,2},{2,1},{3,3},{4,4},{5,6},{6,5},{7,7},{8,8},{9,10},{10,9... | collective-permute-start | bytes 6152 | tf_op jit(solution)/shard_map/ppermute | solution.py:69
  69.3 226.4 %collective-permute-start.7 = (f32[8]{0:T(128)}, f32[8]{0:T(128)}, u32[]{:S(2)}, u32[]{:S(2)}) collective-permute-start(f32[8]{0:T(128)} %bitcast.18), channel_id=1, source_target_pairs={{0,0},{1,2},{2,1},{3,3},{4,4},{5,6},{6,5},{7,7},{8,8},{9,10},{10,9... | collective-permute-start | bytes 104 | tf_op jit(solution)/shard_map/ppermute | solution.py:69
  71.4 13.7 %collective-permute-start = (bf16[32,64,128]{2,1,0:T(8,128)(2,1)S(1)}, bf16[32,64,128]{2,1,0:T(8,128)(2,1)S(1)}, u32[]{:S(2)}, u32[]{:S(2)}) collective-permute-start(bf16[32,64,128]{2,1,0:T(8,128)(2,1)S(1)} %all-to-all-done), channel_id=1, source_target_pairs={{0,2},{2,0},{1,3},{3,1},{4,6},{6,4},{5,7},{7,5},{8,10},{10,8},{9,1... | collective-permute-start | bytes 1572872 | tf_op jit(solution)/shard_map/ppermute | solution.py:74
  71.5 24.8 %collective-permute-start.1 = (bf16[32,64,128]{2,1,0:T(8,128)(2,1)S(1)}, bf16[32,64,128]{2,1,0:T(8,128)(2,1)S(1)}, u32[]{:S(2)}, u32[]{:S(2)}) collective-permute-start(bf16[32,64,128]{2,1,0:T(8,128)(2,1)S(1)} %all-to-all-done), channel_id=1, source_target_pairs={{0,128},{128,0},{1,129},{129,1},{2,130},{130,2},{3,131},{131,3},{4... | collective-permute-start | bytes 1572872 | tf_op jit(solution)/shard_map/ppermute | solution.py:74
  74.3 22.9 %collective-permute-start.2 = (bf16[32,64,128]{2,1,0:T(8,128)(2,1)S(1)}, bf16[32,64,128]{2,1,0:T(8,128)(2,1)S(1)}, u32[]{:S(2)}, u32[]{:S(2)}) collective-permute-start(bf16[32,64,128]{2,1,0:T(8,128)(2,1)S(1)} %all-to-all-done), channel_id=1, source_target_pairs={{0,130},{2,128},{128,2},{130,0},{1,131},{3,129},{129,3},{131,1},{4... | collective-permute-start | bytes 1572872 | tf_op jit(solution)/shard_map/ppermute | solution.py:74
  75.3 209.2 %copy-start.8 = (f32[64]{0:T(128)}, f32[64]{0:T(128)S(1)}, u32[]{:S(2)}) copy-start(f32[64]{0:T(128)S(1)} %multiply_power_fusion) | copy-start | bytes 772
  75.4 229.7 %collective-permute-start.6 = (bf16[512,128]{1,0:T(8,128)(2,1)}, bf16[512,128]{1,0:T(8,128)(2,1)}, u32[]{:S(2)}, u32[]{:S(2)}) collective-permute-start(bf16[512,128]{1,0:T(8,128)(2,1)} %bitcast.17), channel_id=1, source_target_pairs={{0,0},{1,2},{2,1},{3,3},{4,4},{5,6},{6,5},{7,7},{8,8},{9,10},{10,9... | collective-permute-start | bytes 393224 | tf_op jit(solution)/shard_map/ppermute | solution.py:69
  85.0 186.7 %collective-permute-start.5 = (bf16[8,128,256]{2,1,0:T(8,128)(2,1)}, bf16[8,128,256]{2,1,0:T(8,128)(2,1)S(1)}, u32[]{:S(2)}, u32[]{:S(2)}) collective-permute-start(bf16[8,128,256]{2,1,0:T(8,128)(2,1)} %all-to-all-done.2), channel_id=1, source_target_pairs={{0,0},{1,2},{2,1},{3,3},{4,4},{5,6},{6,5},{7,7},{8,8},{9,10},{10,9... | collective-permute-start | bytes 1572872 | tf_op jit(solution)/shard_map/ppermute | solution.py:69
  273.0 17.4 %all-to-all-start.3 = ((f32[8,64,256]{2,1,0:T(8,128)}), f32[8,64,256]{2,1,0:T(8,128)S(1)}, u32[]{:S(2)}, u32[]{:S(2)}) async-start(f32[8,64,256]{2,1,0:T(8,128)} %fusion.55), calls=%async_computation.3 | async-start | bytes 1048576 | tf_op jit(solution)/shard_map/all_to_all | solution.py:78
  291.4 13.0 %all-to-all-start.4 = ((bf16[8,64,256]{2,1,0:T(8,128)(2,1)}), bf16[8,64,256]{2,1,0:T(8,128)(2,1)S(1)}, u32[]{:S(2)}, u32[]{:S(2)}) async-start(bf16[8,64,256]{2,1,0:T(8,128)(2,1)} %broadcast_in_dim.11), calls=%async_computation.4 | async-start | bytes 524288 | tf_op jit(solution)/shard_map/all_to_all | solution.py:78
  326.7 13.1 %all-to-all-start.7 = ((bf16[8,64,256]{2,1,0:T(8,128)(2,1)}), bf16[8,64,256]{2,1,0:T(8,128)(2,1)S(1)}, u32[]{:S(2)}, u32[]{:S(2)}) async-start(bf16[8,64,256]{2,1,0:T(8,128)(2,1)} %broadcast_in_dim.13), calls=%async_computation.7 | async-start | bytes 524288 | tf_op jit(solution)/shard_map/all_to_all | solution.py:78
  341.0 12.0 %all-to-all-start.8 = ((bf16[4,256,256]{2,1,0:T(8,128)(2,1)}), bf16[4,256,256]{2,1,0:T(8,128)(2,1)S(1)}, u32[]{:S(2)}, u32[]{:S(2)}) async-start(bf16[4,256,256]{2,1,0:T(8,128)(2,1)} %bitcast.93), calls=%async_computation.8 | async-start | bytes 1048576 | tf_op jit(solution)/shard_map/all_to_all | solution.py:78
  352.9 28.5 %all-to-all-start.5 = ((bf16[4,2048,128]{2,1,0:T(8,128)(2,1)}), bf16[4,2048,128]{2,1,0:T(8,128)(2,1)}, u32[]{:S(2)}, u32[]{:S(2)}) async-start(bf16[4,2048,128]{2,1,0:T(8,128)(2,1)} %bitcast.19), calls=%async_computation.5 | async-start | bytes 4194304 | tf_op jit(solution)/shard_map/all_to_all | solution.py:78
  400.8 29.0 %all-to-all-start.10 = ((bf16[4,4,256,256]{3,2,1,0:T(8,128)(2,1)}), bf16[4,4,256,256]{3,2,1,0:T(8,128)(2,1)}, u32[]{:S(2)}, u32[]{:S(2)}) async-start(bf16[4,4,256,256]{3,2,1,0:T(8,128)(2,1)} %broadcast_in_dim.15), calls=%async_computation.10 | async-start | bytes 4194304 | tf_op jit(solution)/shard_map/all_to_all | solution.py:78
  429.8 22.9 %collective-permute-start.12 = (bf16[4,4,256,256]{3,2,1,0:T(8,128)(2,1)}, bf16[4,4,256,256]{3,2,1,0:T(8,128)(2,1)}, u32[]{:S(2)}, u32[]{:S(2)}) collective-permute-start(bf16[4,4,256,256]{3,2,1,0:T(8,128)(2,1)} %all-to-all-done.10), channel_id=1, source_target_pairs={{0,1},{1,0},{2,3},{3,2},{4,5},{5,4},{6,7},{7,6},{8,9},{9,8},{10,11... | collective-permute-start | bytes 6291464 | tf_op jit(solution)/shard_map/ppermute | solution.py:74
  432.8 15.5 %collective-permute-start.10 = (bf16[2048,128]{1,0:T(8,128)(2,1)S(1)}, bf16[2048,128]{1,0:T(8,128)(2,1)S(1)}, u32[]{:S(2)}, u32[]{:S(2)}) collective-permute-start(bf16[2048,128]{1,0:T(8,128)(2,1)S(1)} %subtract_convert_fusion), channel_id=1, source_target_pairs={{0,128},{1,130},{2,129},{3,131},{128,0},{129,2},{130,1},{131,3},{4... | collective-permute-start | bytes 1572872 | tf_op jit(solution)/shard_map/ppermute | solution.py:165
  433.6 14.7 %collective-permute-start.8 = (bf16[2048,128]{1,0:T(8,128)(2,1)S(1)}, bf16[2048,128]{1,0:T(8,128)(2,1)S(1)}, u32[]{:S(2)}, u32[]{:S(2)}) collective-permute-start(bf16[2048,128]{1,0:T(8,128)(2,1)S(1)} %subtract_convert_fusion), channel_id=1, source_target_pairs={{0,0},{1,2},{2,1},{3,3},{4,4},{5,6},{6,5},{7,7},{8,8},{9,10},{10,9... | collective-permute-start | bytes 1572872 | tf_op jit(solution)/shard_map/ppermute | solution.py:69
  448.3 1.9 collective-permute-start.11
  448.3 2.7 collective-permute-start.9
  (9 other events, 13.8 us)
